TPU v7x, 128 devices: a whole 4x4x4 slice. The times are simulated.
128 devices in a mesh: date: 8 (over y, core), strip: 16 (over z, x).
Axes of the slice: x: 4, y: 4, z: 4, core: 2. Of those that a mesh axis runs over, the one named last changes fastest.
Arguments:
- stack: float32 [64, 1024, 2048], P('date', 'strip'), may hold values from -6 to 6
- spatial_taps: float32 [13], replicated, may hold values from 0.2 to 1
- temporal_taps: float32 [2, 5], replicated, may hold values from -0.25 to 0.25
- foot_tile: int32 [16384], P(('date', 'strip')), may hold values from 0 to 1
- foot_row: int32 [16384], P(('date', 'strip')), may hold values from 0 to 63
- foot_count: int32 [16384], P(('date', 'strip')), may hold values from 1 to 128
- foot_owner: int32 [16384, 1], P(('date', 'strip')), may hold values from 0 to 127; in each aligned block of 128 rows (0 to 127, 128 to 255, ...) at most 2 rows name the same one
Outputs:
- residual: float32 [64, 1024, 2048], P(None, 'strip', 'date')
- anomaly: float32 [128, 256, 64], P(('date', 'strip'))
- asset_series: float32 [128, 64], P(('date', 'strip'))
Inputs may be any that keep to these rules, and one draw needn't show every extreme that they name: `foot_owner`: among the footprints of one block, no owner appears more than 2 times, a bound that some block reaches; every owner has some footprint.
All inputs are finite; a program needn't handle non-finite values.
Results may differ from a plain program's by a relative error of at most 0.000075.
Values sent between devices are 32-bit elements; how exact they have to be, the bound alone decides.
A program may use at most 128 MiB of HBM per device.

v0:
```python
import jax
import jax.numpy as jnp
from jax import lax
from jax.sharding import PartitionSpec as P

TILE = 128
RADIUS = 6
REACH = 2
DILATION = 8
PAIR_CAP = 2


def with_halo(value, sides, width):
    for axis, dim in sides:
        peers, length = (lax.axis_size(axis), value.shape[dim])
        up = [(i, (i + 1) % peers) for i in range(peers - 1)]
        down = [(j, i) for i, j in up]
        last = lax.slice_in_dim(value, length - width, length, axis=dim)
        initial = lax.slice_in_dim(value, 0, width, axis=dim)
        before = lax.ppermute(last, axis, up)
        after = lax.ppermute(initial, axis, down)
        value = jnp.concatenate([before, value, after], axis=dim)
    return value


def taps_pass(padded, weights, axis_num, length):
    summed = weights[0] * lax.slice_in_dim(padded, 0, length, axis=axis_num)
    for k in range(1, weights.shape[0]):
        summed = summed + weights[k] * lax.slice_in_dim(padded, k, k + length, axis=axis_num)
    return summed


def temporal_filter(series, temporal_taps):
    date_count = series.shape[0]
    for level_idx, spacing in enumerate((1, DILATION)):
        margin = REACH * spacing
        padded = jnp.pad(series, ((margin, margin), (0, 0), (0, 0)))
        smooth_part = temporal_taps[level_idx, 0] * lax.slice_in_dim(padded, 0, date_count, axis=0)
        for k in range(1, 2 * REACH + 1):
            smooth_part = smooth_part + temporal_taps[level_idx, k] * lax.slice_in_dim(
                padded, k * spacing, k * spacing + date_count, axis=0
            )
        series = series - smooth_part
    return series


def shards(stack, spatial_taps, temporal_taps, foot_tile, foot_row, foot_count, foot_owner):
    weights = spatial_taps / jnp.sum(spatial_taps)
    padded = jnp.pad(stack, ((0, 0), (0, 0), (RADIUS, RADIUS)))
    across = taps_pass(padded, weights, 2, stack.shape[2])
    rimmed = with_halo(across, (("strip", 1),), RADIUS)
    corrected = stack - taps_pass(rimmed, weights, 1, stack.shape[1])
    residual = temporal_filter(
        lax.all_to_all(corrected, "date", split_axis=2, concat_axis=0, tiled=True), temporal_taps
    )
    date_count, row_count, col_count = residual.shape
    tile_view = residual.reshape(date_count, row_count, col_count // TILE, TILE)
    picked = tile_view[:, foot_row, foot_tile, :]
    counts = foot_count.astype(jnp.float32)
    inside = (jnp.arange(TILE, dtype=jnp.int32)[None, :] < foot_count[:, None]).astype(jnp.float32)
    foot_mean = jnp.sum(picked * inside[None], axis=2) / counts[None, :]
    owners = foot_owner[:, 0]
    position = jnp.arange(owners.shape[0], dtype=jnp.int32)
    earlier = (owners[:, None] == owners[None, :]) & (position[None, :] < position[:, None])
    slot_rank = jnp.sum(earlier.astype(jnp.int32), axis=1)
    date_devices = lax.axis_size("date")
    strip_devices = lax.axis_size("strip")
    devices_all = date_devices * strip_devices
    dest_slot = owners * PAIR_CAP + slot_rank
    onehot = (
        dest_slot[:, None] == jnp.arange(devices_all * PAIR_CAP, dtype=jnp.int32)[None, :]
    ).astype(jnp.float32)
    outgoing = jnp.einsum("fk,tf->kt", onehot, foot_mean, precision=lax.Precision.HIGHEST)
    out_weight = jnp.einsum("fk,f->k", onehot, counts, precision=lax.Precision.HIGHEST)
    received, weight_in = (
        lax.all_to_all(
            outgoing.reshape(devices_all, PAIR_CAP, date_count),
            ("date", "strip"),
            split_axis=0,
            concat_axis=0,
            tiled=True,
        ),
        lax.all_to_all(
            out_weight.reshape(devices_all, PAIR_CAP),
            ("date", "strip"),
            split_axis=0,
            concat_axis=0,
            tiled=True,
        ),
    )
    total_weight = jnp.sum(weight_in)
    asset_mean = jnp.sum(weight_in[:, :, None] * received, axis=(0, 1)) / total_weight
    anomaly = jnp.where(weight_in[:, :, None] > 0, received - asset_mean[None, None, :], 0.0)
    return (residual, anomaly.reshape(1, devices_all * PAIR_CAP, date_count), asset_mean[None, :])


def solution(mesh):
    placed = (
        P("date", "strip", None),
        P(),
        P(),
        P(("date", "strip")),
        P(("date", "strip")),
        P(("date", "strip")),
        P(("date", "strip"), None),
    )
    return jax.shard_map(
        shards,
        mesh=mesh,
        in_specs=placed,
        out_specs=(
            P(None, "strip", "date"),
            P(("date", "strip"), None, None),
            P(("date", "strip"), None),
        ),
        check_vma=False,
    )
```

profile of v0, /device:TPU:1, one launch (start us, length us, event | category | flops | bytes accessed | tf_op | source)
XLA Modules:
  0.0 279.2 jit_solution(2231093077993058063)
XLA Ops:
  1.9 1.3 broadcast_divide_fusion.1
  3.9 6.6 %copy.37 = f32[8,64,2048]{2,0,1:T(8,128)} copy(f32[8,64,2048]{2,1,0:T(8,128)} %param.7) | data formatting | bytes 8388608 | tf_op args[0]
  10.5 42.0 %multiply_add_fusion = f32[8,64,2048]{2,0,1:T(8,128)} fusion(f32[8,64,2048]{2,0,1:T(8,128)} %copy.37, f32[]{:T(128)} %bitcast.12, f32[]{:T(128)} %bitcast.11, f32[]{:T(128)} %bitcast.10, f32[]{:T(128)} %bitcast.9, f32[]{:T(128)} %bitcast.8, f32[]{:T(128)} %bitcast.7, f32[]{:T(128)} %bitcast.6, f32[]{:T(128)} %bitcast.5, f32[]{:T(128)} %bitcast.4, ...), kind=kLoop, calls=%fused_computation.79 | loop fusion | flops 26214400 | bytes 8388660 | tf_op jit(solution)/shard_map/add | solution.py:29
  53.7 4.0 %collective-permute-start = (f32[8,6,2048]{2,0,1:T(8,128)S(1)}, f32[8,6,2048]{2,0,1:T(8,128)S(1)}, u32[]{:S(2)}, u32[]{:S(2)}) collective-permute-start(f32[8,6,2048]{2,0,1:T(8,128)S(1)} %get-tuple-element.18), channel_id=1, source_target_pairs={{0,1},{1,2},{2,3},{3,4},{4,5},{5,6},{6,7},{7,8},{8,9},{9,10},{10,1... | collective-permute-start | bytes 1179656 | tf_op jit(solution)/shard_map/ppermute | solution.py:20
  57.7 1.5 collective-permute-start.1
  59.2 6.3 %collective-permute-done = f32[8,6,2048]{2,0,1:T(8,128)S(1)} collective-permute-done((f32[8,6,2048]{2,0,1:T(8,128)S(1)}, f32[8,6,2048]{2,0,1:T(8,128)S(1)}, u32[]{:S(2)}, u32[]{:S(2)}) %collective-permute-start) | collective-permute-done | bytes 393248 | tf_op jit(solution)/shard_map/ppermute | solution.py:20
  65.5 3.8 %collective-permute-done.1 = f32[8,6,2048]{2,0,1:T(8,128)S(1)} collective-permute-done((f32[8,6,2048]{2,0,1:T(8,128)S(1)}, f32[8,6,2048]{2,0,1:T(8,128)S(1)}, u32[]{:S(2)}, u32[]{:S(2)}) %collective-permute-start.1) | collective-permute-done | bytes 393248 | tf_op jit(solution)/shard_map/ppermute | solution.py:21
  69.3 32.9 %fusion.4 = f32[8,64,2048]{2,0,1:T(8,128)} fusion(f32[8,64,2048]{2,0,1:T(8,128)} %multiply_add_fusion, f32[8,6,2048]{2,0,1:T(8,128)S(1)} %collective-permute-done.1, f32[8,6,2048]{2,0,1:T(8,128)S(1)} %collective-permute-done, f32[]{:T(128)} %bitcast.12, f32[]{:T(128)} %bitcast.11, f32[]{:T(128)} %bitcast.10, f32[]{:T(128)} %bitcast.9, f32[]{:T(128)} %bitcast.8, ...), kind=kLoop, calls=%fused_computation.29 | loop fusion | flops 39845888 | bytes 13369396 | tf_op jit(solution)/shard_map/sub | solution.py:52
  102.1 7.5 %copy.38 = f32[8,64,2048]{1,0,2:T(8,128)} copy(f32[8,64,2048]{2,0,1:T(8,128)} %fusion.4) | data formatting | bytes 8388608 | tf_op jit(solution)/shard_map/sub | solution.py:52
  109.6 9.8 %reshape.84 = f32[8,1,131072]{2,1,0:T(1,128)} reshape(f32[2048,8,64]{2,1,0:T(8,128)} %bitcast.46) | data formatting | bytes 8388608
  119.5 6.5 %all-to-all-start = ((f32[8,1,131072]{2,1,0:T(1,128)}), f32[8,1,131072]{2,1,0:T(1,128)}, u32[]{:S(2)}, u32[]{:S(2)}) async-start(f32[8,1,131072]{2,1,0:T(1,128)} %reshape.84), calls=%async_computation | async-start | bytes 8388608 | tf_op jit(solution)/shard_map/all_to_all | solution.py:54
  127.9 46.9 %all-to-all-done = f32[8,1,131072]{2,1,0:T(1,128)} async-done(((f32[8,1,131072]{2,1,0:T(1,128)}), f32[8,1,131072]{2,1,0:T(1,128)}, u32[]{:S(2)}, u32[]{:S(2)}) %all-to-all-start) | async-done | bytes 4194336 | tf_op jit(solution)/shard_map/all_to_all | solution.py:54
  174.8 10.6 %all-to-all-start.1 = ((f32[128,1,2]{2,1,0:T(1,128)}), f32[128,1,2]{2,1,0:T(1,128)S(1)}, u32[]{:S(2)}, u32[]{:S(2)}) async-start(f32[128,1,2]{2,1,0:T(1,128)} %bitcast.31), calls=%async_computation.1 | async-start | bytes 131072 | tf_op jit(solution)/shard_map/all_to_all | solution.py:83
  185.9 13.8 %reduce.3 = f32[8,131072]{1,0:T(8,128)} reduce(f32[8,1,131072]{2,1,0:T(1,128)} %all-to-all-done, f32[]{:T(128)} %broadcast.84), dimensions={1}, to_apply=%all_to_all.24.reduce_sub_computation | reduce | bytes 8388612 | tf_op jit(solution)/shard_map/all_to_all | solution.py:54
  199.7 8.7 %reshape.85 = f32[2048,8,64]{2,1,0:T(8,128)} reshape(f32[8,131072]{1,0:T(8,128)} %reduce.3) | data formatting | bytes 8388608
  208.4 6.8 %copy.39 = f32[8,8,64,256]{3,2,1,0:T(8,128)} copy(f32[8,8,64,256]{2,1,3,0:T(8,128)} %bitcast.47) | data formatting | bytes 8388608 | tf_op jit(solution)/shard_map/all_to_all | solution.py:54
  215.1 12.2 %add_subtract_fusion = f32[64,64,256]{2,1,0:T(8,128)S(1)} fusion(f32[64,64,256]{2,1,0:T(8,128)} %bitcast.48, f32[]{:T(128)} %bitcast.20, f32[]{:T(128)} %bitcast.19, f32[]{:T(128)} %bitcast.18, f32[]{:T(128)} %bitcast.17, f32[]{:T(128)} %bitcast.16), kind=kLoop, calls=%fused_computation.72 | loop fusion | flops 10485760 | bytes 8388628 | tf_op jit(solution)/shard_map/sub | solution.py:43
  227.3 6.6 %fusion.38 = f32[64,64,256]{2,1,0:T(8,128)} fusion(f32[64,64,256]{2,1,0:T(8,128)S(1)} %add_subtract_fusion, f32[]{:T(128)} %bitcast.25, f32[]{:T(128)} %bitcast.24, f32[]{:T(128)} %bitcast.23, f32[]{:T(128)} %bitcast.22, f32[]{:T(128)} %bitcast.21), kind=kLoop, calls=%fused_computation.63 | loop fusion | flops 10485760 | bytes 8388628 | tf_op jit(solution)/shard_map/sub | solution.py:43
  233.9 5.8 %reshape.61 = f32[64,64,2,128]{3,2,1,0:T(2,128)} reshape(f32[64,64,256]{2,1,0:T(8,128)} %fusion.38) | data formatting | bytes 8388608 | tf_op jit(solution)/shard_map/reshape | solution.py:57
  239.7 6.5 %copy.41 = f32[64,64,2,128]{3,0,2,1:T(8,128)} copy(f32[64,64,2,128]{3,2,1,0:T(2,128)} %reshape.61) | data formatting | bytes 8388608 | tf_op jit(solution)/shard_map/reshape | solution.py:57
  246.2 5.0 %gather_fusion = f32[128,64,128]{2,1,0:T(8,128)} fusion(f32[64,64,2,128]{3,0,2,1:T(8,128)} %copy.41, s32[128]{0:T(128)S(1)} %fusion.67), kind=kCustom, calls=%fused_computation | custom fusion | bytes 8389632 | tf_op jit(solution)/shard_map/gather | solution.py:58
  251.3 3.4 %multiply_reduce_fusion = f32[128,64]{1,0:T(8,128)S(1)} fusion(f32[128,64,128]{2,1,0:T(8,128)} %gather_fusion, f32[128,128]{1,0:T(8,128)S(1)} %fusion.63), kind=kLoop, calls=%fused_computation.71 | loop fusion | flops 2088960 | bytes 4292608 | tf_op jit(solution)/shard_map/reduce_sum | solution.py:61
  255.8 9.8 %all-to-all-start.2 = ((f32[128,1,128]{2,1,0:T(1,128)}), f32[128,1,128]{2,1,0:T(1,128)S(1)}, u32[]{:S(2)}, u32[]{:S(2)}) async-start(f32[128,1,128]{2,1,0:T(1,128)} %reshape.86), calls=%async_computation.2 | async-start | bytes 131072 | tf_op jit(solution)/shard_map/all_to_all | solution.py:76
  266.4 8.9 %all-to-all-done.2 = f32[128,1,128]{2,1,0:T(1,128)S(1)} async-done(((f32[128,1,128]{2,1,0:T(1,128)}), f32[128,1,128]{2,1,0:T(1,128)S(1)}, u32[]{:S(2)}, u32[]{:S(2)}) %all-to-all-start.2) | async-done | bytes 65568 | tf_op jit(solution)/shard_map/all_to_all | solution.py:76
  (34 shorter events, 11.5 us)
Async XLA Ops:
  53.7 11.7 %collective-permute-start = (f32[8,6,2048]{2,0,1:T(8,128)S(1)}, f32[8,6,2048]{2,0,1:T(8,128)S(1)}, u32[]{:S(2)}, u32[]{:S(2)}) collective-permute-start(f32[8,6,2048]{2,0,1:T(8,128)S(1)} %get-tuple-element.18), channel_id=1, source_target_pairs={{0,1},{1,2},{2,3},{3,4},{4,5},{5,6},{6,7},{7,8},{8,9},{9,10},{10,1... | collective-permute-start | bytes 1179656 | tf_op jit(solution)/shard_map/ppermute | solution.py:20
  57.7 11.6 %collective-permute-start.1 = (f32[8,6,2048]{2,0,1:T(8,128)S(1)}, f32[8,6,2048]{2,0,1:T(8,128)S(1)}, u32[]{:S(2)}, u32[]{:S(2)}) collective-permute-start(f32[8,6,2048]{2,0,1:T(8,128)S(1)} %get-tuple-element.19), channel_id=1, source_target_pairs={{1,0},{2,1},{3,2},{4,3},{5,4},{6,5},{7,6},{8,7},{9,8},{10,9},{11,1... | collective-permute-start | bytes 1179656 | tf_op jit(solution)/shard_map/ppermute | solution.py:21
  119.4 6.5 %copy-start.1 = (s32[128]{0:T(128)S(1)}, s32[128]{0:T(128)}, u32[]{:S(2)}) copy-start(s32[128]{0:T(128)} %param.12) | copy-start | bytes 1540
  119.4 6.5 %copy-start.2 = (s32[128,1]{0,1:T(1,128)S(1)}, s32[128,1]{0,1:T(1,128)}, u32[]{:S(2)}) copy-start(s32[128,1]{0,1:T(1,128)} %param.13) | copy-start | bytes 1540
  119.4 7.7 %copy-start = (f32[2,5]{1,0:T(2,128)S(1)}, f32[2,5]{1,0:T(2,128)}, u32[]{:S(2)}) copy-start(f32[2,5]{1,0:T(2,128)} %param.9) | copy-start | bytes 124
  119.4 8.4 %copy-start.3 = (s32[128]{0:T(128)S(1)}, s32[128]{0:T(128)}, u32[]{:S(2)}) copy-start(s32[128]{0:T(128)} %param.11) | copy-start | bytes 1540
  119.4 8.4 %copy-start.4 = (s32[128]{0:T(128)S(1)}, s32[128]{0:T(128)}, u32[]{:S(2)}) copy-start(s32[128]{0:T(128)} %param.10) | copy-start | bytes 1540
  119.5 55.4 %all-to-all-start = ((f32[8,1,131072]{2,1,0:T(1,128)}), f32[8,1,131072]{2,1,0:T(1,128)}, u32[]{:S(2)}, u32[]{:S(2)}) async-start(f32[8,1,131072]{2,1,0:T(1,128)} %reshape.84), calls=%async_computation | async-start | bytes 8388608 | tf_op jit(solution)/shard_map/all_to_all | solution.py:54
  174.8 80.9 %all-to-all-start.1 = ((f32[128,1,2]{2,1,0:T(1,128)}), f32[128,1,2]{2,1,0:T(1,128)S(1)}, u32[]{:S(2)}, u32[]{:S(2)}) async-start(f32[128,1,2]{2,1,0:T(1,128)} %bitcast.31), calls=%async_computation.1 | async-start | bytes 131072 | tf_op jit(solution)/shard_map/all_to_all | solution.py:83
  255.8 19.5 %all-to-all-start.2 = ((f32[128,1,128]{2,1,0:T(1,128)}), f32[128,1,128]{2,1,0:T(1,128)S(1)}, u32[]{:S(2)}, u32[]{:S(2)}) async-start(f32[128,1,128]{2,1,0:T(1,128)} %reshape.86), calls=%async_computation.2 | async-start | bytes 131072 | tf_op jit(solution)/shard_map/all_to_all | solution.py:76
where the time goes:
time: 281 us; the launch traced here: 279 us
  other arithmetic  118 us (42%)
  waiting for transfers between devices  65.9 us (23%)
  local copies, waits for them, and re-layouts  62.2 us (22%)
  starting transfers between devices  32.2 us (11%)
    all_to_all x1, waiting for transfers between devices, shards(): lax.all_to_all(corrected, 'date', split_axis=2, concat_axis=0, tiled=True)  46.9 us
    add x1, other arithmetic, taps_pass(): summed + weights[k] * lax.slice_in_dim(padded, k, k + length, axis=axis_num)  42 us
    sub x1, other arithmetic, shards(): corrected = stack - taps_pass(rimmed, weights, 1, stack.shape[1])  32.9 us
    unnamed x16, local copies, waits for them, and re-layouts  26.8 us
    sub x2, other arithmetic, temporal_filter(): series = series - smooth_part  18.8 us
    all_to_all x1, other arithmetic, shards(): lax.all_to_all(corrected, 'date', split_axis=2, concat_axis=0, tiled=True)  13.8 us
    reshape x2, local copies, waits for them, and re-layouts, shards(): tile_view = residual.reshape(date_count, row_count, col_count // TILE, TILE)  12.3 us
    all_to_all x1, starting transfers between devices, shards(): lax.all_to_all(out_weight.reshape(devices_all, PAIR_CAP), ('date', 'strip...  10.6 us
  transfers between devices with their start and end apart: 5, of which 4 were waited for; matrix products, arithmetic and copies ran while one was open for 26% of the time, Pallas kernels for 0%

commit v1 on v0

--- a/solution.py
+++ b/solution.py
@@ -51,7 +51,13 @@
     rimmed = with_halo(across, (("strip", 1),), RADIUS)
     corrected = stack - taps_pass(rimmed, weights, 1, stack.shape[1])
     residual = temporal_filter(
-        lax.all_to_all(corrected, "date", split_axis=2, concat_axis=0, tiled=True), temporal_taps
+        jnp.concatenate(
+            lax.all_to_all(
+                jnp.stack(jnp.split(corrected, lax.axis_size("date"), axis=2)), "date", 0, 0
+            ),
+            axis=0,
+        ),
+        temporal_taps,
     )
     date_count, row_count, col_count = residual.shape
     tile_view = residual.reshape(date_count, row_count, col_count // TILE, TILE)

time: 281 us -> 242 us (0.86)
  local copies, waits for them, and re-layouts: 62.2 us -> 29.6 us
  other arithmetic: 118 us -> 110 us
  waiting for transfers between devices: 65.9 us -> 68.8 us
    unnamed x16 -> x20, local copies, waits for them, and re-layouts: 26.8 us -> 7.48 us
    all_to_all x1 -> x0, other arithmetic: 13.8 us -> none  [shards(): lax.all_to_all(corrected, 'date', split_axis=2, concat_axis=0, tiled=True)]
    sub x1 -> x0, local copies, waits for them, and re-layouts: 7.48 us -> none  [shards(): corrected = stack - taps_pass(rimmed, weights, 1, stack.shape[1])]
    all_to_all x2 -> x1, local copies, waits for them, and re-layouts: 7.29 us -> 0.51 us  [shards(): lax.all_to_all(outgoing.reshape(devices_all, PAIR_CAP, date_count), ('dat...]
    sub x1, other arithmetic: 32.9 us -> 38.8 us  [shards(): corrected = stack - taps_pass(rimmed, weights, 1, stack.shape[1])]
    ppermute x1, waiting for transfers between devices: 6.26 us -> 9.24 us  [with_halo(): before = lax.ppermute(last, axis, up)]
  transfers between devices with their start and end apart: 5 -> 5, of which waited for: 4 -> 4; matrix products, arithmetic and copies ran while one was open for 26% -> 18% of each run, Pallas kernels for 0% -> 0%
where the time goes in v1:
time: 242 us; the launch traced here: 241 us
  other arithmetic  110 us (45%)
  waiting for transfers between devices  68.8 us (28%)
  starting transfers between devices  32.1 us (13%)
  local copies, waits for them, and re-layouts  29.6 us (12%)
    all_to_all x1, waiting for transfers between devices, shards(): lax.all_to_all(jnp.stack(jnp.split(corrected, lax.axis_size('date'), axis...  46.9 us
    add x1, other arithmetic, taps_pass(): summed + weights[k] * lax.slice_in_dim(padded, k, k + length, axis=axis_num)  41.8 us
    sub x1, other arithmetic, shards(): corrected = stack - taps_pass(rimmed, weights, 1, stack.shape[1])  38.8 us
    sub x2, other arithmetic, temporal_filter(): series = series - smooth_part  18.8 us
    reshape x2, local copies, waits for them, and re-layouts, shards(): tile_view = residual.reshape(date_count, row_count, col_count // TILE, TILE)  12.3 us
    all_to_all x1, starting transfers between devices, shards(): lax.all_to_all(out_weight.reshape(devices_all, PAIR_CAP), ('date', 'strip...  10.5 us
    all_to_all x1, starting transfers between devices, shards(): lax.all_to_all(outgoing.reshape(devices_all, PAIR_CAP, date_count), ('dat...  9.76 us
    ppermute x1, waiting for transfers between devices, with_halo(): before = lax.ppermute(last, axis, up)  9.24 us
  transfers between devices with their start and end apart: 5, of which 4 were waited for; matrix products, arithmetic and copies ran while one was open for 18% of the time, Pallas kernels for 0%

profile of v1, /device:TPU:1, one launch (start us, length us, event | category | flops | bytes accessed | tf_op | source)
XLA Modules:
  0.0 241.4 jit_solution(9381639222899346599)
XLA Ops:
  0.6 1.3 reduce_sum.47
  1.9 1.3 broadcast_divide_fusion.1
  3.9 41.8 %multiply_add_fusion = f32[8,64,2048]{2,1,0:T(8,128)} fusion(f32[8,64,2048]{2,1,0:T(8,128)} %param.7, f32[]{:T(128)} %bitcast.12, f32[]{:T(128)} %bitcast.11, f32[]{:T(128)} %bitcast.10, f32[]{:T(128)} %bitcast.9, f32[]{:T(128)} %bitcast.8, f32[]{:T(128)} %bitcast.7, f32[]{:T(128)} %bitcast.6, f32[]{:T(128)} %bitcast.5, f32[]{:T(128)} %bitcast.4, ...), kind=kLoop, calls=%fused_computation.79 | loop fusion | flops 26214400 | bytes 8388660 | tf_op jit(solution)/shard_map/add | solution.py:29
  45.7 1.3 fusion.81
  47.0 4.0 %collective-permute-start = (f32[8,6,2048]{2,1,0:T(8,128)S(1)}, f32[8,6,2048]{2,1,0:T(8,128)S(1)}, u32[]{:S(2)}, u32[]{:S(2)}) collective-permute-start(f32[8,6,2048]{2,1,0:T(8,128)S(1)} %get-tuple-element.15), channel_id=1, source_target_pairs={{0,1},{1,2},{2,3},{3,4},{4,5},{5,6},{6,7},{7,8},{8,9},{9,10},{10,1... | collective-permute-start | bytes 1179656 | tf_op jit(solution)/shard_map/ppermute | solution.py:20
  50.9 1.3 collective-permute-start.1
  52.2 9.2 %collective-permute-done = f32[8,6,2048]{2,1,0:T(8,128)S(1)} collective-permute-done((f32[8,6,2048]{2,1,0:T(8,128)S(1)}, f32[8,6,2048]{2,1,0:T(8,128)S(1)}, u32[]{:S(2)}, u32[]{:S(2)}) %collective-permute-start) | collective-permute-done | bytes 393248 | tf_op jit(solution)/shard_map/ppermute | solution.py:20
  61.5 3.8 %collective-permute-done.1 = f32[8,6,2048]{2,1,0:T(8,128)S(1)} collective-permute-done((f32[8,6,2048]{2,1,0:T(8,128)S(1)}, f32[8,6,2048]{2,1,0:T(8,128)S(1)}, u32[]{:S(2)}, u32[]{:S(2)}) %collective-permute-start.1) | collective-permute-done | bytes 393248 | tf_op jit(solution)/shard_map/ppermute | solution.py:21
  65.3 38.8 %fusion.4 = f32[8,64,2048]{2,1,0:T(8,128)S(1)} fusion(f32[8,64,2048]{2,1,0:T(8,128)} %param.7, f32[8,64,2048]{2,1,0:T(8,128)} %multiply_add_fusion, f32[8,6,2048]{2,1,0:T(8,128)S(1)} %collective-permute-done.1, f32[8,6,2048]{2,1,0:T(8,128)S(1)} %collective-permute-done, f32[]{:T(128)} %bitcast.12, f32[]{:T(128)} %bitcast.11, f32[]{:T(128)} %bitcast.10, ...), kind=kLoop, calls=%fused_computation.29 | loop fusion | flops 39845888 | bytes 13369396 | tf_op jit(solution)/shard_map/sub | solution.py:52
  104.9 0.8 fusion.63
  105.8 0.8 fusion.62
  108.3 0.8 fusion.59
  110.8 6.5 %all-to-all-start = ((f32[8,8,64,256]{3,2,1,0:T(8,128)}), f32[8,8,64,256]{3,2,1,0:T(8,128)}, u32[]{:S(2)}, u32[]{:S(2)}) async-start(f32[8,8,64,256]{3,2,1,0:T(8,128)} %fusion.57), calls=%async_computation | async-start | bytes 8388608 | tf_op jit(solution)/shard_map/all_to_all | solution.py:55
  119.3 46.9 %all-to-all-done = f32[8,8,64,256]{3,2,1,0:T(8,128)} async-done(((f32[8,8,64,256]{3,2,1,0:T(8,128)}), f32[8,8,64,256]{3,2,1,0:T(8,128)}, u32[]{:S(2)}, u32[]{:S(2)}) %all-to-all-start) | async-done | bytes 4194336 | tf_op jit(solution)/shard_map/all_to_all | solution.py:55
  166.2 10.5 %all-to-all-start.1 = ((f32[128,1,2]{2,1,0:T(1,128)}), f32[128,1,2]{2,1,0:T(1,128)S(1)}, u32[]{:S(2)}, u32[]{:S(2)}) async-start(f32[128,1,2]{2,1,0:T(1,128)} %bitcast.37), calls=%async_computation.1 | async-start | bytes 131072 | tf_op jit(solution)/shard_map/all_to_all | solution.py:89
  176.7 12.1 %add_subtract_fusion = f32[64,64,256]{2,1,0:T(8,128)S(1)} fusion(f32[64,64,256]{2,1,0:T(8,128)} %bitcast.21, f32[]{:T(128)} %bitcast.26, f32[]{:T(128)} %bitcast.25, f32[]{:T(128)} %bitcast.24, f32[]{:T(128)} %bitcast.23, f32[]{:T(128)} %bitcast.22), kind=kLoop, calls=%fused_computation.72 | loop fusion | flops 10485760 | bytes 8388628 | tf_op jit(solution)/shard_map/sub | solution.py:43
  188.9 6.7 %fusion.38 = f32[64,64,256]{2,1,0:T(8,128)} fusion(f32[64,64,256]{2,1,0:T(8,128)S(1)} %add_subtract_fusion, f32[]{:T(128)} %bitcast.31, f32[]{:T(128)} %bitcast.30, f32[]{:T(128)} %bitcast.29, f32[]{:T(128)} %bitcast.28, f32[]{:T(128)} %bitcast.27), kind=kLoop, calls=%fused_computation.63 | loop fusion | flops 10485760 | bytes 8388628 | tf_op jit(solution)/shard_map/sub | solution.py:43
  195.6 5.8 %reshape.65 = f32[64,64,2,128]{3,2,1,0:T(2,128)} reshape(f32[64,64,256]{2,1,0:T(8,128)} %fusion.38) | data formatting | bytes 8388608 | tf_op jit(solution)/shard_map/reshape | solution.py:63
  201.3 6.5 %copy.20 = f32[64,64,2,128]{3,0,2,1:T(8,128)} copy(f32[64,64,2,128]{3,2,1,0:T(2,128)} %reshape.65) | data formatting | bytes 8388608 | tf_op jit(solution)/shard_map/reshape | solution.py:63
  207.9 5.0 %gather_fusion = f32[128,64,128]{2,1,0:T(8,128)} fusion(f32[64,64,2,128]{3,0,2,1:T(8,128)} %copy.20, s32[128]{0:T(128)S(1)} %fusion.75), kind=kCustom, calls=%fused_computation | custom fusion | bytes 8389632 | tf_op jit(solution)/shard_map/gather | solution.py:64
  212.9 3.4 %multiply_reduce_fusion = f32[128,64]{1,0:T(8,128)S(1)} fusion(f32[128,64,128]{2,1,0:T(8,128)} %gather_fusion, f32[128,128]{1,0:T(8,128)S(1)} %fusion.71), kind=kLoop, calls=%fused_computation.71 | loop fusion | flops 2088960 | bytes 4292608 | tf_op jit(solution)/shard_map/reduce_sum | solution.py:67
  217.4 9.8 %all-to-all-start.2 = ((f32[128,1,128]{2,1,0:T(1,128)}), f32[128,1,128]{2,1,0:T(1,128)S(1)}, u32[]{:S(2)}, u32[]{:S(2)}) async-start(f32[128,1,128]{2,1,0:T(1,128)} %reshape.88), calls=%async_computation.2 | async-start | bytes 131072 | tf_op jit(solution)/shard_map/all_to_all | solution.py:82
  228.0 8.9 %all-to-all-done.2 = f32[128,1,128]{2,1,0:T(1,128)S(1)} async-done(((f32[128,1,128]{2,1,0:T(1,128)}), f32[128,1,128]{2,1,0:T(1,128)S(1)}, u32[]{:S(2)}, u32[]{:S(2)}) %all-to-all-start.2) | async-done | bytes 65568 | tf_op jit(solution)/shard_map/all_to_all | solution.py:82
  239.3 1.2 fusion.84
  (36 shorter events, 12.1 us)
Async XLA Ops:
  47.0 14.5 %collective-permute-start = (f32[8,6,2048]{2,1,0:T(8,128)S(1)}, f32[8,6,2048]{2,1,0:T(8,128)S(1)}, u32[]{:S(2)}, u32[]{:S(2)}) collective-permute-start(f32[8,6,2048]{2,1,0:T(8,128)S(1)} %get-tuple-element.15), channel_id=1, source_target_pairs={{0,1},{1,2},{2,3},{3,4},{4,5},{5,6},{6,7},{7,8},{8,9},{9,10},{10,1... | collective-permute-start | bytes 1179656 | tf_op jit(solution)/shard_map/ppermute | solution.py:20
  50.9 14.4 %collective-permute-start.1 = (f32[8,6,2048]{2,1,0:T(8,128)S(1)}, f32[8,6,2048]{2,1,0:T(8,128)S(1)}, u32[]{:S(2)}, u32[]{:S(2)}) collective-permute-start(f32[8,6,2048]{2,1,0:T(8,128)S(1)} %get-tuple-element.16), channel_id=1, source_target_pairs={{1,0},{2,1},{3,2},{4,3},{5,4},{6,5},{7,6},{8,7},{9,8},{10,9},{11,1... | collective-permute-start | bytes 1179656 | tf_op jit(solution)/shard_map/ppermute | solution.py:21
  110.8 6.5 %copy-start.1 = (s32[128]{0:T(128)S(1)}, s32[128]{0:T(128)}, u32[]{:S(2)}) copy-start(s32[128]{0:T(128)} %param.12) | copy-start | bytes 1540
  110.8 6.5 %copy-start.2 = (s32[128,1]{0,1:T(1,128)S(1)}, s32[128,1]{0,1:T(1,128)}, u32[]{:S(2)}) copy-start(s32[128,1]{0,1:T(1,128)} %param.13) | copy-start | bytes 1540
  110.8 7.7 %copy-start = (f32[2,5]{1,0:T(2,128)S(1)}, f32[2,5]{1,0:T(2,128)}, u32[]{:S(2)}) copy-start(f32[2,5]{1,0:T(2,128)} %param.9) | copy-start | bytes 124
  110.8 8.4 %copy-start.3 = (s32[128]{0:T(128)S(1)}, s32[128]{0:T(128)}, u32[]{:S(2)}) copy-start(s32[128]{0:T(128)} %param.11) | copy-start | bytes 1540
  110.8 8.4 %copy-start.4 = (s32[128]{0:T(128)S(1)}, s32[128]{0:T(128)}, u32[]{:S(2)}) copy-start(s32[128]{0:T(128)} %param.10) | copy-start | bytes 1540
  110.8 55.4 %all-to-all-start = ((f32[8,8,64,256]{3,2,1,0:T(8,128)}), f32[8,8,64,256]{3,2,1,0:T(8,128)}, u32[]{:S(2)}, u32[]{:S(2)}) async-start(f32[8,8,64,256]{3,2,1,0:T(8,128)} %fusion.57), calls=%async_computation | async-start | bytes 8388608 | tf_op jit(solution)/shard_map/all_to_all | solution.py:55
  166.2 51.2 %all-to-all-start.1 = ((f32[128,1,2]{2,1,0:T(1,128)}), f32[128,1,2]{2,1,0:T(1,128)S(1)}, u32[]{:S(2)}, u32[]{:S(2)}) async-start(f32[128,1,2]{2,1,0:T(1,128)} %bitcast.37), calls=%async_computation.1 | async-start | bytes 131072 | tf_op jit(solution)/shard_map/all_to_all | solution.py:89
  217.4 19.5 %all-to-all-start.2 = ((f32[128,1,128]{2,1,0:T(1,128)}), f32[128,1,128]{2,1,0:T(1,128)S(1)}, u32[]{:S(2)}, u32[]{:S(2)}) async-start(f32[128,1,128]{2,1,0:T(1,128)} %reshape.88), calls=%async_computation.2 | async-start | bytes 131072 | tf_op jit(solution)/shard_map/all_to_all | solution.py:82
